TPU v7x, 32 devices: a whole 2x2x4 slice. The times are simulated.
32 devices in a mesh: dp: 8 (over y, x, core), mp: 4 (over z).
Axes of the slice: x: 2, y: 2, z: 4, core: 2. Of those that a mesh axis runs over, the one named last changes fastest.
Arguments:
- patches: bfloat16 [8192, 1024], P(('dp', 'mp')), as said below
- scene_ids: int32 [8192], P(('dp', 'mp')), may hold values from 0 to 7, as said below
- owner_ids: int32 [8192], P(('dp', 'mp')), may hold values from 0 to 7, as said below
- fill_slot: int32 [32768], P(('dp', 'mp')), may hold values from -1 to 511, as said below
- norm1_gain: float32 [1024], replicated, may hold values from 0.1 to 1.9
- norm1_bias: float32 [1024], replicated, may hold values from -1.75 to 1.75
- qkv_weight: bfloat16 [1024, 3, 1024], P(None, None, 'mp'), may hold values from -0.25 to 0.25
- qv_bias: float32 [2, 1024], P(None, 'mp'), may hold values from -3 to 3
- out_weight: bfloat16 [1024, 1024], P('mp'), may hold values from -1.5 to 1.5
- out_bias: float32 [1024], replicated, may hold values from -1.75 to 1.75
- norm2_gain: float32 [1024], replicated, may hold values from 0.1 to 1.9
- norm2_bias: float32 [1024], replicated, may hold values from -1.75 to 1.75
- up_weight: bfloat16 [1024, 4096], P(None, 'mp'), may hold values from -0.1875 to 0.1875
- up_bias: bfloat16 [4096], P('mp'), may hold values from -3 to 3
- down_weight: bfloat16 [4096, 1024], P('mp'), may hold values from -0.125 to 0.125
- down_bias: float32 [1024], replicated, may hold values from -1.75 to 1.75
- dec_weight: bfloat16 [1024, 512], replicated, may hold values from -0.1875 to 0.1875
- dec_bias: float32 [512], replicated, may hold values from -1.75 to 1.75
- mask_token: float32 [512], replicated, may hold values from -6 to 6
- positions: bfloat16 [32768, 512], P(('dp', 'mp')), may hold values from -6 to 6
- cotangent: bfloat16 [32768, 512], P(('dp', 'mp')), may hold values from -6 to 6
Outputs:
- decoder_in: bfloat16 [32768, 512], P(('dp', 'mp'))
- grad_patches: float32 [8192, 1024], P(('dp', 'mp'))
- grad_norm1_gain: float32 [1024], replicated
- grad_norm1_bias: float32 [1024], replicated
- grad_qkv_weight: float32 [1024, 3, 1024], P(None, None, 'mp')
- grad_qv_bias: float32 [2, 1024], P(None, 'mp')
- grad_out_weight: float32 [1024, 1024], P('mp')
- grad_out_bias: float32 [1024], replicated
- grad_norm2_gain: float32 [1024], replicated
- grad_norm2_bias: float32 [1024], replicated
- grad_up_weight: float32 [1024, 4096], P(None, 'mp')
- grad_up_bias: float32 [4096], P('mp')
- grad_down_weight: float32 [4096, 1024], P('mp')
- grad_down_bias: float32 [1024], replicated
- grad_dec_weight: float32 [1024, 512], replicated
- grad_dec_bias: float32 [512], replicated
- grad_mask_token: float32 [512], replicated
Inputs may be any that keep to these rules, and one draw needn't show every extreme that they name: `scene_ids`: within each group of 1024 rows (one dp index) scene ids start at 0 and rise by one at each scene boundary, never falling; scene 0 holds 256 to 512 rows, every other scene at least one. `owner_ids`: among the 256 rows of one device no owner is named more than 64 times; in each mp column one owner is named exactly 64 times by the rows of every device. `fill_slot`: in grid block e, slot s * 64 + r is named by exactly one cell when device (s, e % 4) has an r-th row (in row order) with owner e // 4, and by no cell otherwise. `patches`: magnitudes stay below 200.
All inputs are finite; a program needn't handle non-finite values.
Results may differ from a plain program's by a relative error of at most 0.013.
The roundings to bfloat16 on the way count: a program that leaves them out, or rounds other values in their place, can miss the bound.
Values may be sent and summed in bfloat16 or wider, within the bound.
A program may use at most 128 MiB of HBM per device.

v0:
```python
import jax
import jax.numpy as jnp
from jax import lax
from jax.sharding import PartitionSpec as P

HEAD_DIM = 64
QBLOCK = 512


NEG_FILL = -1000000000.0


def layer_norm(hidden, gain, bias_vec):
    centered = hidden - jnp.mean(hidden, axis=-1, keepdims=True)
    spread = jnp.mean(centered * centered, axis=-1, keepdims=True)
    return centered * lax.rsqrt(spread + 1e-06) * gain + bias_vec


def gelu_exact(values):
    return jax.nn.gelu(values, approximate=False)


def per_device(
    patches,
    scene_ids,
    owner_ids,
    fill_slot,
    norm1_gain,
    norm1_bias,
    qkv_weight,
    qv_bias,
    out_weight,
    out_bias,
    norm2_gain,
    norm2_bias,
    up_weight,
    up_bias,
    down_weight,
    down_bias,
    dec_weight,
    dec_bias,
    mask_token,
    positions,
    cotangent,
):
    row_count = patches.shape[0]
    model_par = lax.axis_size("mp")
    data_par = lax.axis_size("dp")
    group_rows = row_count * model_par
    total_rows = float(row_count * model_par * data_par)
    local_width = qkv_weight.shape[2]
    local_heads = local_width // HEAD_DIM
    score_scale = HEAD_DIM ** (-0.5)
    block_rows = min(QBLOCK, group_rows)
    block_starts = jnp.arange(group_rows // block_rows, dtype=jnp.int32) * block_rows
    capacity = 2 * row_count // data_par
    slot_count = capacity * data_par
    dec_width = dec_weight.shape[1]
    inputs_f = patches.astype(jnp.float32)
    band_sums = lax.psum(
        (jnp.sum(inputs_f, axis=0), jnp.sum(inputs_f * inputs_f, axis=0)), ("dp", "mp")
    )
    band_mean = band_sums[0] / total_rows
    band_var = band_sums[1] / total_rows - band_mean * band_mean
    band_scale = lax.rsqrt(band_var + 1e-05)
    band_hat = (inputs_f - band_mean) * band_scale
    normed1 = layer_norm(band_hat, norm1_gain, norm1_bias).astype(jnp.bfloat16)
    norm1_all, scene_all = (
        lax.all_gather(normed1, "mp", axis=0, tiled=True),
        lax.all_gather(scene_ids, "mp", axis=0, tiled=True),
    )
    bias_three = jnp.stack([qv_bias[0], jnp.zeros_like(qv_bias[0]), qv_bias[1]])
    triples = (
        jnp.einsum("td,dcj->tcj", norm1_all, qkv_weight, preferred_element_type=jnp.float32)
        + bias_three
    ).astype(jnp.bfloat16)
    query_all = triples[:, 0].reshape(group_rows, local_heads, HEAD_DIM)
    key_all = triples[:, 1].reshape(group_rows, local_heads, HEAD_DIM)
    value_all = triples[:, 2].reshape(group_rows, local_heads, HEAD_DIM)

    def block_scores(first_row):
        query_blk = lax.dynamic_slice_in_dim(query_all, first_row, block_rows, 0)
        scene_blk = lax.dynamic_slice_in_dim(scene_all, first_row, block_rows, 0)
        scores = (
            jnp.einsum("qhd,khd->hqk", query_blk, key_all, preferred_element_type=jnp.float32)
            * score_scale
        )
        same_scene = (scene_blk[:, None] == scene_all[None, :])[None]
        return (jnp.where(same_scene, scores, NEG_FILL), query_blk)

    def attend_block(first_row):
        scores, query_blk = block_scores(first_row)
        row_max = jnp.max(scores, axis=-1, keepdims=True)
        exp_scores = jnp.exp(scores - row_max)
        row_total = jnp.sum(exp_scores, axis=-1, keepdims=True)
        softmax_w = (exp_scores / row_total).astype(jnp.bfloat16)
        mixed_rows = jnp.einsum(
            "hqk,khd->qhd", softmax_w, value_all, preferred_element_type=jnp.float32
        )
        return (mixed_rows.astype(jnp.bfloat16), (row_max + jnp.log(row_total))[..., 0])

    head_blocks, lse_blocks = lax.map(attend_block, block_starts)
    heads_out = head_blocks.reshape(group_rows, local_width)
    piece = heads_out
    attn_local = lax.psum_scatter(
        jnp.dot(piece, out_weight, preferred_element_type=jnp.float32),
        "mp",
        scatter_dimension=0,
        tiled=True,
    )
    after_attn = band_hat + attn_local + out_bias
    normed2 = layer_norm(after_attn, norm2_gain, norm2_bias).astype(jnp.bfloat16)
    norm2_all = lax.all_gather(normed2, "mp", axis=0, tiled=True)
    pre_act = jnp.dot(norm2_all, up_weight, preferred_element_type=jnp.float32) + up_bias.astype(
        jnp.float32
    )
    act_rows = gelu_exact(pre_act).astype(jnp.bfloat16)
    piece = act_rows
    mlp_local = lax.psum_scatter(
        jnp.dot(piece, down_weight, preferred_element_type=jnp.float32),
        "mp",
        scatter_dimension=0,
        tiled=True,
    )
    block_out = after_attn + mlp_local + down_bias
    encoded = block_out.astype(jnp.bfloat16)
    projected = (
        jnp.dot(encoded, dec_weight, preferred_element_type=jnp.float32) + dec_bias
    ).astype(jnp.bfloat16)
    owner_onehot = (owner_ids[:, None] == jnp.arange(data_par, dtype=jnp.int32)[None, :]).astype(
        jnp.int32
    )
    earlier = jnp.sum((jnp.cumsum(owner_onehot, axis=0) - owner_onehot) * owner_onehot, axis=1)
    send_slot = owner_ids * capacity + earlier
    slot_range = jnp.arange(slot_count, dtype=jnp.int32)
    send_onehot = (send_slot[:, None] == slot_range[None, :]).astype(jnp.bfloat16)
    outgoing = jnp.einsum(
        "rs,rc->sc", send_onehot, projected, preferred_element_type=jnp.float32
    ).astype(jnp.bfloat16)
    fill_onehot = (fill_slot[:, None] == slot_range[None, :]).astype(jnp.bfloat16)
    returning = jnp.einsum(
        "gs,gc->sc", fill_onehot, cotangent, preferred_element_type=jnp.float32
    ).astype(jnp.bfloat16)
    arrived, grad_back = (
        lax.all_to_all(
            outgoing.reshape(data_par, capacity, dec_width),
            "dp",
            split_axis=0,
            concat_axis=0,
            tiled=True,
        ),
        lax.all_to_all(
            returning.reshape(data_par, capacity, dec_width),
            "dp",
            split_axis=0,
            concat_axis=0,
            tiled=True,
        ),
    )
    placed = jnp.dot(
        fill_onehot, arrived.reshape(slot_count, dec_width), preferred_element_type=jnp.float32
    )
    masked = (fill_slot < 0)[:, None]
    decoder_in = (jnp.where(masked, mask_token, placed) + positions.astype(jnp.float32)).astype(
        jnp.bfloat16
    )
    grad_mask_local = jnp.sum(jnp.where(masked, cotangent.astype(jnp.float32), 0.0), axis=0)
    grad_proj = jnp.einsum(
        "rs,sc->rc",
        send_onehot,
        grad_back.reshape(slot_count, dec_width),
        preferred_element_type=jnp.float32,
    )
    grad_proj_low = grad_proj.astype(jnp.bfloat16)
    grad_dec_local = jnp.einsum(
        "rd,rc->dc", encoded, grad_proj_low, preferred_element_type=jnp.float32
    )
    grad_dec_bias_local = jnp.sum(grad_proj, axis=0)
    grad_block = jnp.einsum(
        "rc,dc->rd", grad_proj_low, dec_weight, preferred_element_type=jnp.float32
    )
    grad_mlp = grad_block.astype(jnp.bfloat16)
    grad_down_bias_local = jnp.sum(grad_mlp.astype(jnp.float32), axis=0)
    grad_mlp_all = lax.all_gather(grad_mlp, "mp", axis=0, tiled=True)
    grad_act = jnp.einsum(
        "tc,fc->tf", grad_mlp_all, down_weight, preferred_element_type=jnp.float32
    )
    grad_down_local = jnp.einsum(
        "tf,tc->fc", act_rows, grad_mlp_all, preferred_element_type=jnp.float32
    )
    gelu_val, gelu_back = jax.vjp(gelu_exact, pre_act)
    grad_pre = gelu_back(grad_act)[0].astype(jnp.bfloat16)
    grad_up_local = jnp.einsum("td,tf->df", norm2_all, grad_pre, preferred_element_type=jnp.float32)
    grad_up_bias_local = jnp.sum(grad_pre.astype(jnp.float32), axis=0)
    piece = grad_pre
    grad_norm2 = lax.psum_scatter(
        jnp.einsum("tf,df->td", piece, up_weight, preferred_element_type=jnp.float32),
        "mp",
        scatter_dimension=0,
        tiled=True,
    )
    norm2_val, norm2_back = jax.vjp(layer_norm, after_attn, norm2_gain, norm2_bias)
    from_norm2, grad_gain2_local, grad_bias2_local = norm2_back(grad_norm2)
    grad_after = grad_block + from_norm2
    grad_attn = grad_after.astype(jnp.bfloat16)
    grad_out_bias_local = jnp.sum(grad_attn.astype(jnp.float32), axis=0)
    grad_attn_all = lax.all_gather(grad_attn, "mp", axis=0, tiled=True)
    grad_out_local = jnp.einsum(
        "tj,tc->jc", heads_out, grad_attn_all, preferred_element_type=jnp.float32
    )
    grad_heads = jnp.einsum(
        "tc,jc->tj", grad_attn_all, out_weight, preferred_element_type=jnp.float32
    ).astype(jnp.bfloat16)
    grad_heads3 = grad_heads.reshape(group_rows, local_heads, HEAD_DIM)

    def back_block(carried, inputs):
        key_acc, value_acc = carried
        first_row, log_total = inputs
        scores, query_blk = block_scores(first_row)
        softmax_w = jnp.exp(scores - log_total[..., None])
        upstream = lax.dynamic_slice_in_dim(grad_heads3, first_row, block_rows, 0)
        value_acc = value_acc + jnp.einsum(
            "hqk,qhd->khd",
            softmax_w.astype(jnp.bfloat16),
            upstream,
            preferred_element_type=jnp.float32,
        )
        grad_probs = jnp.einsum(
            "qhd,khd->hqk", upstream, value_all, preferred_element_type=jnp.float32
        )
        inner_sum = jnp.sum(softmax_w * grad_probs, axis=-1, keepdims=True)
        grad_scores = (softmax_w * (grad_probs - inner_sum)).astype(jnp.bfloat16)
        grad_query = (
            jnp.einsum("hqk,khd->qhd", grad_scores, key_all, preferred_element_type=jnp.float32)
            * score_scale
        )
        key_acc = (
            key_acc
            + jnp.einsum("hqk,qhd->khd", grad_scores, query_blk, preferred_element_type=jnp.float32)
            * score_scale
        )
        return ((key_acc, value_acc), grad_query.astype(jnp.bfloat16))

    zero_heads = jnp.zeros((group_rows, local_heads, HEAD_DIM), jnp.float32)
    (key_grad, value_grad), query_blocks = lax.scan(
        back_block, (zero_heads, zero_heads), (block_starts, lse_blocks)
    )
    grad_triples = jnp.stack(
        [
            query_blocks.reshape(group_rows, local_width),
            key_grad.reshape(group_rows, local_width).astype(jnp.bfloat16),
            value_grad.reshape(group_rows, local_width).astype(jnp.bfloat16),
        ],
        axis=1,
    )
    grad_qkv_local = jnp.einsum(
        "td,tcj->dcj", norm1_all, grad_triples, preferred_element_type=jnp.float32
    )
    triple_sums = jnp.sum(grad_triples.astype(jnp.float32), axis=0)
    grad_qv_local = jnp.stack([triple_sums[0], triple_sums[2]])
    piece = grad_triples
    grad_norm1 = lax.psum_scatter(
        jnp.einsum("tcj,dcj->td", piece, qkv_weight, preferred_element_type=jnp.float32),
        "mp",
        scatter_dimension=0,
        tiled=True,
    )
    norm1_val, norm1_back = jax.vjp(layer_norm, band_hat, norm1_gain, norm1_bias)
    from_norm1, grad_gain1_local, grad_bias1_local = norm1_back(grad_norm1)
    grad_hat = grad_after + from_norm1
    summed_weights = lax.psum(
        (
            grad_qkv_local,
            grad_qv_local,
            grad_out_local,
            grad_up_local,
            grad_up_bias_local,
            grad_down_local,
        ),
        "dp",
    )
    shared = lax.psum(
        (
            jnp.sum(grad_hat, axis=0),
            jnp.sum(grad_hat * band_hat, axis=0),
            grad_gain1_local,
            grad_bias1_local,
            grad_gain2_local,
            grad_bias2_local,
            grad_out_bias_local,
            grad_down_bias_local,
            grad_dec_local,
            grad_dec_bias_local,
            grad_mask_local,
        ),
        ("dp", "mp"),
    )
    grad_patches = band_scale * (
        grad_hat - shared[0] / total_rows - band_hat * (shared[1] / total_rows)
    )
    return (
        decoder_in,
        grad_patches,
        shared[2],
        shared[3],
        summed_weights[0],
        summed_weights[1],
        summed_weights[2],
        shared[6],
        shared[4],
        shared[5],
        summed_weights[3],
        summed_weights[4],
        summed_weights[5],
        shared[7],
        shared[8],
        shared[9],
        shared[10],
    )


def solution(mesh):
    in_specs = (
        P(("dp", "mp"), None),
        P(("dp", "mp")),
        P(("dp", "mp")),
        P(("dp", "mp")),
        P(),
        P(),
        P(None, None, "mp"),
        P(None, "mp"),
        P("mp", None),
        P(),
        P(),
        P(),
        P(None, "mp"),
        P("mp"),
        P("mp", None),
        P(),
        P(),
        P(),
        P(),
        P(("dp", "mp"), None),
        P(("dp", "mp"), None),
    )
    out_specs = (
        P(("dp", "mp"), None),
        P(("dp", "mp"), None),
        P(),
        P(),
        P(None, None, "mp"),
        P(None, "mp"),
        P("mp", None),
        P(),
        P(),
        P(),
        P(None, "mp"),
        P("mp"),
        P("mp", None),
        P(),
        P(),
        P(),
        P(),
    )
    return jax.shard_map(
        per_device, mesh=mesh, in_specs=in_specs, out_specs=out_specs, check_vma=False
    )
```

profile of v0, /device:TPU:0, one launch (start us, length us, event | category | flops | bytes accessed | tf_op | source)
XLA Modules:
  0.0 991.9 jit_solution(5100809643732990345)
XLA Ops:
  8.6 42.1 %all-reduce.1 = (f32[1024]{0:T(1024)S(1)}, f32[1024]{0:T(1024)S(1)}) all-reduce(f32[1024]{0:T(1024)S(1)} %get-tuple-element.170, f32[1024]{0:T(1024)S(1)} %get-tuple-element.169), channel_id=1, replica_groups=mesh['dp'=8,'mp'=4] {'dp','mp'}, use_global_device_ids=true, to_apply=%region_6.7 | all-reduce | flops 2048 | bytes 16384 | tf_op jit(solution)/shard_map/psum | solution.py:60
  55.7 10.0 %all-gather = s32[4,1,256]{2,1,0:T(1,128)S(1)} all-gather(s32[1,1,256]{2,1,0:T(1,128)} %bitcast.144), channel_id=1, replica_groups=mesh['dp'=8,'mp'=4] {'mp'}, dimensions={0}, use_global_device_ids=true | all-gather | bytes 5120 | tf_op jit(solution)/shard_map/all_gather | solution.py:70
  66.5 34.7 %all-gather.6.cloned.1.call-done = bf16[1024,1024]{1,0:T(8,128)(2,1)} async-done(((bf16[256,1024]{1,0:T(8,128)(2,1)}), bf16[1024,1024]{1,0:T(8,128)(2,1)}) %all-gather.6.cloned.1.call-update) | async-done | bytes 2097168 | tf_op jit(solution)/shard_map/all_gather | solution.py:69
  101.2 3.9 add_convert_fusion.1
  106.8 22.3 %while.27 = (s32[]{:T(128)}, bf16[2,512,4,64]{1,3,2,0:T(8,128)(2,1)}, f32[2,4,512]{2,1,0:T(4,128)S(1)}, s32[2]{0:T(128)S(1)}, s32[1024]{0:T(1024)S(1)}, /*index=...) while((s32[]{:T(128)}, ...), condition=%wide.region_12.13_spmd, body=%wide.region_9.12_spmd.sunk | while | flops 562690048 | bytes 35203332 | solution.py:102
  111.8 2.3 fusion.168
  114.2 3.0 fusion.169
  125.3 3.0 fusion.169
  131.8 3.8 fusion.104
  135.7 75.7 %reduce-scatter.5.cloned.1.call-done = f32[256,1024]{1,0:T(8,128)} async-done(((f32[1024,1024]{1,0:T(8,128)}), f32[256,1024]{1,0:T(8,128)}) %reduce-scatter.5.cloned.1.call-update) | async-done | bytes 1048592 | tf_op jit(solution)/shard_map/reduce_scatter | solution.py:105
  215.0 3.0 fusion.52
  218.0 3.7 all-to-all-start.1
  223.2 8.2 all-to-all-done.1
  233.1 3.4 convert_reduce_fusion.3
  236.6 24.7 %all-gather.8.cloned.1.call-done = bf16[1024,1024]{1,0:T(8,128)(2,1)} async-done(((bf16[256,1024]{1,0:T(8,128)(2,1)}), bf16[1024,1024]{1,0:T(8,128)(2,1)}) %all-gather.8.cloned.1.call-update) | async-done | bytes 2097168 | tf_op jit(solution)/shard_map/all_gather | solution.py:113
  261.3 6.6 fusion.105
  267.9 39.9 %all-gather.10.cloned.1.call-done = bf16[1024,1024]{1,0:T(8,128)(2,1)} async-done(((bf16[256,1024]{1,0:T(8,128)(2,1)}), bf16[1024,1024]{1,0:T(8,128)(2,1)}) %all-gather.10.cloned.1.call-update) | async-done | bytes 2097168 | tf_op jit(solution)/shard_map/all_gather | solution.py:184
  307.8 15.4 %convert_reduce_fusion = (f32[1024]{0:T(1024)}, bf16[1024,1024]{1,0:T(8,128)(2,1)S(1)}, f32[1024,1024]{1,0:T(8,128)}) fusion(f32[1024,1024]{1,0:T(8,128)} %fusion.105, f32[1024]{0:T(1024)S(1)} %convert_element_type.128, bf16[1024,1024]{1,0:T(8,128)(2,1)} %all-gather.10.cloned.1.call-done, bf16[1024,1024]{1,0:T(8,128)(2,1)S(1)} %copy-done), kind=kOutput, calls=%fused_computation.47 | convolution fusion | flops 2226125824 | bytes 14688256 | tf_op jit(solution)/shard_map/tc,fc->tf/dot_general | solution.py:185
  324.5 4.3 fusion.107
  328.9 4.6 multiply_convert_fusion.1
  334.8 4.4 fusion.106
  339.4 65.2 %reduce-scatter.9.cloned.1.call-done = f32[256,1024]{1,0:T(8,128)} async-done(((f32[1024,1024]{1,0:T(8,128)}), f32[256,1024]{1,0:T(8,128)}) %reduce-scatter.9.cloned.1.call-update) | async-done | bytes 1048592 | tf_op jit(solution)/shard_map/reduce_scatter | solution.py:196
  406.2 78.4 %reduce-scatter.7.cloned.1.call-done = f32[256,1024]{1,0:T(8,128)} async-done(((f32[1024,1024]{1,0:T(8,128)}), f32[256,1024]{1,0:T(8,128)}) %reduce-scatter.7.cloned.1.call-update) | async-done | bytes 1048592 | tf_op jit(solution)/shard_map/reduce_scatter | solution.py:119
  484.7 2.7 fusion.97
  488.6 46.3 %all-gather.12.cloned.1.call-done = bf16[1024,1024]{1,0:T(8,128)(2,1)} async-done(((bf16[256,1024]{1,0:T(8,128)(2,1)}), bf16[1024,1024]{1,0:T(8,128)(2,1)}) %all-gather.12.cloned.1.call-update) | async-done | bytes 2097168 | tf_op jit(solution)/shard_map/all_gather | solution.py:207
  534.9 2.4 convolution_convert_fusion
  538.2 30.4 %while.28 = (s32[]{:T(128)}, f32[1024,4,64]{0,2,1:T(8,128)S(1)}, f32[1024,4,64]{0,2,1:T(8,128)}, bf16[2,512,4,64]{1,3,2,0:T(8,128)(2,1)}, s32[2]{0:T(128)S(1)}, ...) while((s32[]{:T(128)}, f32[1024,4,64]{0,2,1:T(8,128)S(1)}, ...), condition=%wide.region_22.23_spmd.clone, body=%wide.region_20.22_spmd.clone.sunk | while | flops 1375729664 | bytes 84740432 | solution.py:245
  542.6 2.6 fusion.181
  545.2 3.3 multiply_reduce_fusion.5
  548.5 2.4 multiply_convert_fusion.3
  557.8 2.6 fusion.181
  560.4 3.3 multiply_reduce_fusion.5
  563.7 2.4 multiply_convert_fusion.3
  573.9 5.2 convolution_bitcast_fusion
  580.7 5.9 fusion.110
  588.5 6.8 fusion.109
  597.0 3.6 fusion.44
  603.5 3.8 all-to-all-start
  607.7 9.4 all-to-all-done
  617.8 3.4 add_convert_fusion.2
  622.8 13.0 %all-reduce.2 = (f32[2,256]{1,0:T(2,128)}, f32[1024]{0:T(1024)}) all-reduce(f32[2,256]{1,0:T(2,128)S(1)} %pad_maximum_fusion.2, f32[1024]{0:T(1024)S(1)} %copy-done.58), channel_id=1, replica_groups=mesh['dp'=8,'mp'=4] {'dp'}, use_global_device_ids=true, to_apply=%region_36.37 | all-reduce | flops 1536 | bytes 12288 | tf_op jit(solution)/shard_map/psum | solution.py:271
  635.7 19.1 %reduce-scatter.11.cloned.1.call-done = f32[256,1024]{1,0:T(8,128)} async-done(((f32[1024,1024]{1,0:T(8,128)}), f32[256,1024]{1,0:T(8,128)}) %reduce-scatter.11.cloned.1.call-update) | async-done | bytes 1048592 | tf_op jit(solution)/shard_map/reduce_scatter | solution.py:262
  658.4 2.8 fusion.94
  661.2 42.1 %all-reduce = (f32[1024]{0:T(1024)S(1)}, f32[1024]{0:T(1024)S(1)}, f32[1024]{0:T(1024)}, f32[1024]{0:T(1024)}, f32[1024]{0:T(1024)}, /*index=5*/f32[1024]{0:T(10...) all-reduce(f32[1024]{0:T(1024)S(1)} %get-tuple-element.168, ...), channel_id=1, replica_groups=mesh['dp'=8,'mp'=4] {'dp','mp'}, use_global_device_ids=true, to_apply=%region_29.30 | all-reduce | flops 9216 | bytes 73728 | tf_op jit(solution)/shard_map/psum | solution.py:282
  703.3 2.5 fusion.74
  705.8 90.1 %all-reduce.7.cloned.1.call-done = f32[1024,512]{1,0:T(8,128)} async-done(((f32[1024,512]{1,0:T(8,128)}), f32[1024,512]{1,0:T(8,128)}) %all-reduce.7.cloned.1.call-update) | async-done | bytes 2097168 | tf_op jit(solution)/shard_map/psum | solution.py:282
  795.8 175.8 %all-reduce.9.cloned.1.call-done = (f32[1024,3,256]{2,0,1:T(8,128)}, f32[256,1024]{1,0:T(8,128)}, f32[1024,1024]{1,0:T(8,128)}, f32[1024,1024]{1,0:T(8,128)}) async-done(((f32[1024,3,256]{2,0,1:T(8,128)}, f32[256,1024]{1,0:T(8,128)}, f32[1024,1024]{1,0:T(8,128)}, f32[1024,1024]{1,0:T(8,128)}), (f32[1024,3,256]{2,0,1:T(8,128)}, f32[256,1024]{1,0:T(8,128)}, f32[1024,1024]{1,0:T(8,128)}, ...) | async-done | bytes 12582928 | tf_op jit(solution)/shard_map/psum | solution.py:271
  971.6 3.9 copy.92
  (257 shorter events, 73.0 us)
Async XLA Ops:
  7.2 300.6 %copy-start = (bf16[1024,1024]{1,0:T(8,128)(2,1)S(1)}, bf16[1024,1024]{1,0:T(8,128)(2,1)}, u32[]{:S(2)}) copy-start(bf16[1024,1024]{1,0:T(8,128)(2,1)} %param.39) | copy-start | bytes 6291460
  7.2 94.0 %all-gather.6.cloned.1.call-start = ((), (), s32[]{:S(2)}) async-start(), calls=%async_computation.6 | async-start | bytes 2621440 | tf_op jit(solution)/shard_map/all_gather | solution.py:69
  50.7 160.7 %copy-start.40 = (f32[1024]{0:T(1024)}, f32[1024]{0:T(1024)S(1)}, u32[]{:S(2)}) copy-start(f32[1024]{0:T(1024)S(1)} %get-tuple-element.249) | copy-start | bytes 12292
  50.7 160.7 %copy-start.42 = (f32[1024]{0:T(1024)}, f32[1024]{0:T(1024)S(1)}, u32[]{:S(2)}) copy-start(f32[1024]{0:T(1024)S(1)} %get-tuple-element.250) | copy-start | bytes 12292
  52.0 49.2 %copy-start.46 = (f32[256]{0:T(256)}, f32[256]{0:T(256)S(1)}, u32[]{:S(2)}) copy-start(f32[256]{0:T(256)S(1)} %broadcast_multiply_fusion.4) | copy-start | bytes 3076
  53.3 47.8 %copy-start.51 = (f32[256]{0:T(256)}, f32[256]{0:T(256)S(1)}, u32[]{:S(2)}) copy-start(f32[256]{0:T(256)S(1)} %fusion.69) | copy-start | bytes 3076
  53.4 47.8 %copy-start.49 = (f32[256]{0:T(256)}, f32[256]{0:T(256)S(1)}, u32[]{:S(2)}) copy-start(f32[256]{0:T(256)S(1)} %fusion.90) | copy-start | bytes 3076
  55.5 155.9 %reduce-scatter.5.cloned.1.call-start = ((), (), s32[]{:S(2)}) async-start(), calls=%async_computation.7 | async-start | bytes 5242880 | tf_op jit(solution)/shard_map/reduce_scatter | solution.py:105
  135.6 75.8 %copy-start.2 = (bf16[256,1024]{1,0:T(8,128)(2,1)S(1)}, bf16[256,1024]{1,0:T(8,128)(2,1)}, u32[]{:S(2)}) copy-start(bf16[256,1024]{1,0:T(8,128)(2,1)} %param.25) | copy-start | bytes 1572868
  135.6 75.8 %copy-start.54 = (f32[1024]{0:T(1024)S(1)}, f32[1024]{0:T(1024)}, u32[]{:S(2)}) copy-start(f32[1024]{0:T(1024)} %param.34) | copy-start | bytes 12292
  135.6 78.3 %copy-start.45 = (f32[1024]{0:T(1024)S(1)}, f32[1024]{0:T(1024)}, u32[]{:S(2)}) copy-start(f32[1024]{0:T(1024)} %param.35) | copy-start | bytes 12292
  135.6 78.3 %copy-start.55 = (f32[1024]{0:T(1024)S(1)}, f32[1024]{0:T(1024)}, u32[]{:S(2)}) copy-start(f32[1024]{0:T(1024)} %param.36) | copy-start | bytes 12292
  135.6 79.4 %copy-start.56 = (s32[1024]{0:T(1024)S(1)}, s32[1024]{0:T(1024)}, u32[]{:S(2)}) copy-start(s32[1024]{0:T(1024)} %param.28) | copy-start | bytes 12292
  135.7 125.7 %all-gather.8.cloned.1.call-start = ((), (), s32[]{:S(2)}) async-start(), calls=%async_computation.8 | async-start | bytes 2621440 | tf_op jit(solution)/shard_map/all_gather | solution.py:113
  213.0 9.2 copy-start.53
  215.0 21.6 %copy-start.60 = (bf16[1024]{0:T(1024)(128)(2,1)S(1)}, bf16[1024]{0:T(1024)(128)(2,1)}, u32[]{:S(2)}) copy-start(bf16[1024]{0:T(1024)(128)(2,1)} %param.38) | copy-start | bytes 6148
  218.0 13.4 %all-to-all-start.1 = ((bf16[8,64,512]{2,1,0:T(8,128)(2,1)}), bf16[8,64,512]{2,1,0:T(8,128)(2,1)S(1)}, u32[]{:S(2)}, u32[]{:S(2)}) async-start(bf16[8,64,512]{2,1,0:T(8,128)(2,1)} %bitcast.140), calls=%async_computation.3 | async-start | bytes 1048576 | tf_op jit(solution)/shard_map/all_to_all | solution.py:152
  221.7 86.1 %all-gather.10.cloned.1.call-start = ((), (), s32[]{:S(2)}) async-start(), calls=%async_computation.10 | async-start | bytes 2621440 | tf_op jit(solution)/shard_map/all_gather | solution.py:184
  223.2 44.7 %copy-start.62 = (s32[256]{0:T(256)}, s32[256]{0:T(256)S(1)}, u32[]{:S(2)}) copy-start(s32[256]{0:T(256)S(1)} %multiply_add_fusion.2) | copy-start | bytes 3076
  236.5 168.1 %reduce-scatter.9.cloned.1.call-start = ((), (), s32[]{:S(2)}) async-start(), calls=%async_computation.11 | async-start | bytes 5242880 | tf_op jit(solution)/shard_map/reduce_scatter | solution.py:196
  307.8 16.7 %copy-start.64 = (bf16[1024,1024]{1,0:T(8,128)(2,1)S(1)}, bf16[1024,1024]{1,0:T(8,128)(2,1)}, u32[]{:S(2)}) copy-start(bf16[1024,1024]{1,0:T(8,128)(2,1)} %param.37) | copy-start | bytes 6291460
  328.9 155.8 %reduce-scatter.7.cloned.1.call-start = ((), (), s32[]{:S(2)}) async-start(), calls=%async_computation.9 | async-start | bytes 5242880 | tf_op jit(solution)/shard_map/reduce_scatter | solution.py:119
  339.2 65.4 %copy-start.7 = (f32[256,1024]{1,0:T(8,128)S(1)}, f32[256,1024]{1,0:T(8,128)}, u32[]{:S(2)}) copy-start(f32[256,1024]{1,0:T(8,128)} %copy-done.6) | copy-start | bytes 3145732
  339.2 145.5 %copy-start.59 = (f32[1024]{0:T(1024)S(1)}, f32[1024]{0:T(1024)}, u32[]{:S(2)}) copy-start(f32[1024]{0:T(1024)} %param.40) | copy-start | bytes 12292
  339.2 148.2 %copy-start.10 = (f32[256,1024]{1,0:T(8,128)S(1)}, f32[256,1024]{1,0:T(8,128)}, u32[]{:S(2)}) copy-start(f32[256,1024]{1,0:T(8,128)} %get-tuple-element.253) | copy-start | bytes 3145732
  339.2 195.7 %all-gather.12.cloned.1.call-start = ((), (), s32[]{:S(2)}) async-start(), calls=%async_computation.12 | async-start | bytes 2621440 | tf_op jit(solution)/shard_map/all_gather | solution.py:207
  488.5 49.6 %copy-start.5 = (bf16[1024,4,64]{0,2,1:T(8,128)(2,1)S(1)}, bf16[1024,4,64]{0,2,1:T(8,128)(2,1)}, u32[]{:S(2)}) copy-start(bf16[1024,4,64]{0,2,1:T(8,128)(2,1)} %copy-done.4) | copy-start | bytes 1572868
  488.6 49.6 %copy-start.9 = (bf16[1024,4,64]{0,2,1:T(8,128)(2,1)S(1)}, bf16[1024,4,64]{0,2,1:T(8,128)(2,1)}, u32[]{:S(2)}) copy-start(bf16[1024,4,64]{0,2,1:T(8,128)(2,1)} %get-tuple-element.497) | copy-start | bytes 1572868
  488.6 166.3 %reduce-scatter.11.cloned.1.call-start = ((), (), s32[]{:S(2)}) async-start(), calls=%async_computation.13 | async-start | bytes 5242880 | tf_op jit(solution)/shard_map/reduce_scatter | solution.py:262
  579.2 216.7 %all-reduce.7.cloned.1.call-start = ((), (), s32[]{:S(2)}) async-start(), calls=%async_computation.14 | async-start | bytes 4194304 | tf_op jit(solution)/shard_map/psum | solution.py:282
  588.5 383.2 %all-reduce.9.cloned.1.call-start = ((), (), s32[]{:S(2)}) async-start(), calls=%async_computation.15 | async-start | bytes 25165824 | tf_op jit(solution)/shard_map/psum | solution.py:271
  588.5 8.5 copy-start.22
  588.5 8.5 copy-start.24
  588.5 8.5 copy-start.65
  602.0 15.9 %copy-start.67 = (f32[512]{0:T(512)S(1)}, f32[512]{0:T(512)}, u32[]{:S(2)}) copy-start(f32[512]{0:T(512)} %param.43) | copy-start | bytes 6148
  603.5 19.3 %copy-start.58 = (f32[1024]{0:T(1024)S(1)}, f32[1024]{0:T(1024)}, u32[]{:S(2)}) copy-start(f32[1024]{0:T(1024)} %get-tuple-element.227) | copy-start | bytes 12292
  603.5 51.4 %copy-start.3 = (bf16[256,1024]{1,0:T(8,128)(2,1)S(1)}, bf16[256,1024]{1,0:T(8,128)(2,1)}, u32[]{:S(2)}) copy-start(bf16[256,1024]{1,0:T(8,128)(2,1)} %param.25) | copy-start | bytes 1572868
  603.5 51.4 %copy-start.41 = (f32[1024]{0:T(1024)S(1)}, f32[1024]{0:T(1024)}, u32[]{:S(2)}) copy-start(f32[1024]{0:T(1024)} %copy-done.40) | copy-start | bytes 12292
  603.5 51.4 %copy-start.43 = (f32[1024]{0:T(1024)S(1)}, f32[1024]{0:T(1024)}, u32[]{:S(2)}) copy-start(f32[1024]{0:T(1024)} %copy-done.42) | copy-start | bytes 12292
  603.5 51.4 %copy-start.44 = (f32[1024]{0:T(1024)S(1)}, f32[1024]{0:T(1024)}, u32[]{:S(2)}) copy-start(f32[1024]{0:T(1024)} %param.29) | copy-start | bytes 12292
  603.5 51.4 %copy-start.47 = (f32[256]{0:T(256)S(1)}, f32[256]{0:T(256)}, u32[]{:S(2)}) copy-start(f32[256]{0:T(256)} %copy-done.46) | copy-start | bytes 3076
  603.5 13.5 %all-to-all-start = ((bf16[8,64,512]{2,1,0:T(8,128)(2,1)}), bf16[8,64,512]{2,1,0:T(8,128)(2,1)S(1)}, u32[]{:S(2)}, u32[]{:S(2)}) async-start(bf16[8,64,512]{2,1,0:T(8,128)(2,1)} %bitcast.142), calls=%async_computation.2 | async-start | bytes 1048576 | tf_op jit(solution)/shard_map/all_to_all | solution.py:145
  607.3 49.2 %copy-start.52 = (f32[256]{0:T(256)S(1)}, f32[256]{0:T(256)}, u32[]{:S(2)}) copy-start(f32[256]{0:T(256)} %copy-done.51) | copy-start | bytes 3076
  607.4 49.2 %copy-start.50 = (f32[256]{0:T(256)S(1)}, f32[256]{0:T(256)}, u32[]{:S(2)}) copy-start(f32[256]{0:T(256)} %copy-done.49) | copy-start | bytes 3076
  617.8 40.5 %copy-start.11 = (f32[256,1024]{1,0:T(8,128)S(1)}, f32[256,1024]{1,0:T(8,128)}, u32[]{:S(2)}) copy-start(f32[256,1024]{1,0:T(8,128)} %get-tuple-element.253) | copy-start | bytes 3145732
  617.8 40.6 %copy-start.13 = (f32[256,1024]{1,0:T(8,128)S(1)}, f32[256,1024]{1,0:T(8,128)}, u32[]{:S(2)}) copy-start(f32[256,1024]{1,0:T(8,128)} %copy-done.12) | copy-start | bytes 3145732
  622.7 38.5 %copy-start.48 = (f32[1024]{0:T(1024)S(1)}, f32[1024]{0:T(1024)}, u32[]{:S(2)}) copy-start(f32[1024]{0:T(1024)} %get-tuple-element.230) | copy-start | bytes 12292
  622.7 38.5 %copy-start.61 = (f32[512]{0:T(512)S(1)}, f32[512]{0:T(512)}, u32[]{:S(2)}) copy-start(f32[512]{0:T(512)} %get-tuple-element.254) | copy-start | bytes 6148
  (40 other events, 106.5 us)
Sparse Core Ops, SparseCore 0:
  55.7 45.4 all-gather.5
  135.8 75.5 reduce-scatter.4
  215.1 46.1 all-gather.7
  263.3 44.4 all-gather.9
  329.0 75.5 reduce-scatter.8
  407.3 77.2 reduce-scatter.6
  488.7 46.1 all-gather.11
  579.3 75.5 reduce-scatter.10
  660.2 135.5 all-reduce.6
  800.8 170.7 all-reduce.8
where the time goes:
time: 1000 us; the launch traced here: 992 us
  waiting for transfers between devices  668 us (67%)
  blocking collectives  107 us (11%)
  matrix products  107 us (11%)
  other arithmetic  42.7 us (4%)
  local copies, waits for them, and re-layouts  35.1 us (4%)
  between operations  15.2 us (2%)
    psum x1, waiting for transfers between devices, per_device(): lax.psum((grad_qkv_local, grad_qv_local, grad_out_local, grad_up_local, g...  176 us
    psum x1, waiting for transfers between devices, per_device(): lax.psum((jnp.sum(grad_hat, axis=0), jnp.sum(grad_hat * band_hat, axis=0)...  90.1 us
    reduce_scatter x1, waiting for transfers between devices, per_device(): lax.psum_scatter(jnp.dot(piece, down_weight, preferred_element_type=jnp.f...  78.4 us
    reduce_scatter x1, waiting for transfers between devices, per_device(): lax.psum_scatter(jnp.dot(piece, out_weight, preferred_element_type=jnp.fl...  75.7 us
    reduce_scatter x1, waiting for transfers between devices, per_device(): lax.psum_scatter(jnp.einsum('tf,df->td', piece, up_weight, preferred_elem...  65.2 us
    all_gather x1, waiting for transfers between devices, per_device(): grad_attn_all = lax.all_gather(grad_attn, 'mp', axis=0, tiled=True)  46.3 us
    psum x1, blocking collectives, per_device(): lax.psum((jnp.sum(inputs_f, axis=0), jnp.sum(inputs_f * inputs_f, axis=0)...  42.1 us
    psum x1, blocking collectives, per_device(): lax.psum((jnp.sum(grad_hat, axis=0), jnp.sum(grad_hat * band_hat, axis=0)...  42.1 us
  transfers between devices with their start and end apart: 12, of which 12 were waited for; matrix products, arithmetic and copies ran while one was open for 6% of the time, Pallas kernels for 0%

commit v1 on v0

--- a/solution.py
+++ b/solution.py
@@ -18,6 +18,19 @@
 
 def gelu_exact(values):
     return jax.nn.gelu(values, approximate=False)
+
+
+def gather_rows(weight, data_par, model_par):
+    rows, width = weight.shape
+    part = rows // data_par
+    mine = lax.dynamic_slice_in_dim(weight, lax.axis_index("dp") * part, part, 0)
+    column = lax.all_gather(mine, "mp", axis=0)
+    whole = lax.all_gather(column, "dp", axis=0)
+    return whole.transpose(1, 0, 2, 3).reshape(model_par * rows, width)
+
+
+def low(values):
+    return values.astype(jnp.bfloat16)
 
 
 def per_device(
@@ -56,6 +69,7 @@
     capacity = 2 * row_count // data_par
     slot_count = capacity * data_par
     dec_width = dec_weight.shape[1]
+    out_full = gather_rows(out_weight, data_par, model_par)
     inputs_f = patches.astype(jnp.float32)
     band_sums = lax.psum(
         (jnp.sum(inputs_f, axis=0), jnp.sum(inputs_f * inputs_f, axis=0)), ("dp", "mp")
@@ -101,13 +115,8 @@
 
     head_blocks, lse_blocks = lax.map(attend_block, block_starts)
     heads_out = head_blocks.reshape(group_rows, local_width)
-    piece = heads_out
-    attn_local = lax.psum_scatter(
-        jnp.dot(piece, out_weight, preferred_element_type=jnp.float32),
-        "mp",
-        scatter_dimension=0,
-        tiled=True,
-    )
+    heads_rows = lax.all_to_all(heads_out, "mp", split_axis=0, concat_axis=1, tiled=True)
+    attn_local = jnp.dot(heads_rows, out_full, preferred_element_type=jnp.float32)
     after_attn = band_hat + attn_local + out_bias
     normed2 = layer_norm(after_attn, norm2_gain, norm2_bias).astype(jnp.bfloat16)
     norm2_all = lax.all_gather(normed2, "mp", axis=0, tiled=True)
@@ -115,18 +124,15 @@
         jnp.float32
     )
     act_rows = gelu_exact(pre_act).astype(jnp.bfloat16)
-    piece = act_rows
-    mlp_local = lax.psum_scatter(
-        jnp.dot(piece, down_weight, preferred_element_type=jnp.float32),
-        "mp",
-        scatter_dimension=0,
-        tiled=True,
-    )
-    block_out = after_attn + mlp_local + down_bias
-    encoded = block_out.astype(jnp.bfloat16)
-    projected = (
-        jnp.dot(encoded, dec_weight, preferred_element_type=jnp.float32) + dec_bias
-    ).astype(jnp.bfloat16)
+    mlp_part = low(jnp.dot(act_rows, down_weight, preferred_element_type=jnp.float32))
+    proj_part = jnp.dot(mlp_part, dec_weight, preferred_element_type=jnp.float32)
+    proj_sum = lax.psum_scatter(low(proj_part), "mp", scatter_dimension=0, tiled=True)
+    direct = after_attn + down_bias
+    projected = low(
+        jnp.dot(low(direct), dec_weight, preferred_element_type=jnp.float32)
+        + proj_sum.astype(jnp.float32)
+        + dec_bias
+    )
     owner_onehot = (owner_ids[:, None] == jnp.arange(data_par, dtype=jnp.int32)[None, :]).astype(
         jnp.int32
     )
@@ -172,45 +178,54 @@
         preferred_element_type=jnp.float32,
     )
     grad_proj_low = grad_proj.astype(jnp.bfloat16)
+    proj_grad_all = lax.all_gather(grad_proj_low, "mp", axis=0, tiled=True)
     grad_dec_local = jnp.einsum(
-        "rd,rc->dc", encoded, grad_proj_low, preferred_element_type=jnp.float32
-    )
+        "rd,rc->dc", low(direct), grad_proj_low, preferred_element_type=jnp.float32
+    ) + jnp.einsum("rd,rc->dc", mlp_part, proj_grad_all, preferred_element_type=jnp.float32)
     grad_dec_bias_local = jnp.sum(grad_proj, axis=0)
     grad_block = jnp.einsum(
         "rc,dc->rd", grad_proj_low, dec_weight, preferred_element_type=jnp.float32
     )
-    grad_mlp = grad_block.astype(jnp.bfloat16)
-    grad_down_bias_local = jnp.sum(grad_mlp.astype(jnp.float32), axis=0)
-    grad_mlp_all = lax.all_gather(grad_mlp, "mp", axis=0, tiled=True)
+    grad_down_bias_local = jnp.sum(low(grad_block).astype(jnp.float32), axis=0)
+    grad_mlp_all = low(
+        jnp.einsum("rc,dc->rd", proj_grad_all, dec_weight, preferred_element_type=jnp.float32)
+    )
     grad_act = jnp.einsum(
         "tc,fc->tf", grad_mlp_all, down_weight, preferred_element_type=jnp.float32
     )
     grad_down_local = jnp.einsum(
         "tf,tc->fc", act_rows, grad_mlp_all, preferred_element_type=jnp.float32
     )
+    down_sum = lax.psum(low(grad_down_local), "dp").astype(jnp.float32)
     gelu_val, gelu_back = jax.vjp(gelu_exact, pre_act)
     grad_pre = gelu_back(grad_act)[0].astype(jnp.bfloat16)
     grad_up_local = jnp.einsum("td,tf->df", norm2_all, grad_pre, preferred_element_type=jnp.float32)
     grad_up_bias_local = jnp.sum(grad_pre.astype(jnp.float32), axis=0)
-    piece = grad_pre
     grad_norm2 = lax.psum_scatter(
-        jnp.einsum("tf,df->td", piece, up_weight, preferred_element_type=jnp.float32),
+        low(jnp.einsum("tf,df->td", grad_pre, up_weight, preferred_element_type=jnp.float32)),
         "mp",
         scatter_dimension=0,
         tiled=True,
-    )
+    ).astype(jnp.float32)
+    up_sum = lax.psum(low(grad_up_local), "dp").astype(jnp.float32)
     norm2_val, norm2_back = jax.vjp(layer_norm, after_attn, norm2_gain, norm2_bias)
     from_norm2, grad_gain2_local, grad_bias2_local = norm2_back(grad_norm2)
     grad_after = grad_block + from_norm2
     grad_attn = grad_after.astype(jnp.bfloat16)
     grad_out_bias_local = jnp.sum(grad_attn.astype(jnp.float32), axis=0)
-    grad_attn_all = lax.all_gather(grad_attn, "mp", axis=0, tiled=True)
-    grad_out_local = jnp.einsum(
-        "tj,tc->jc", heads_out, grad_attn_all, preferred_element_type=jnp.float32
-    )
-    grad_heads = jnp.einsum(
-        "tc,jc->tj", grad_attn_all, out_weight, preferred_element_type=jnp.float32
-    ).astype(jnp.bfloat16)
+    grad_out_rows = low(
+        jnp.einsum("tj,tc->jc", heads_rows, grad_attn, preferred_element_type=jnp.float32)
+    ).reshape(model_par, local_width, -1)
+    out_part = lax.psum_scatter(grad_out_rows, "dp", scatter_dimension=1, tiled=True)
+    out_part = lax.psum_scatter(out_part, "mp", scatter_dimension=0, tiled=True)
+    out_sum = lax.all_gather(out_part[0], "dp", axis=0, tiled=True).astype(jnp.float32)
+    grad_heads = lax.all_to_all(
+        low(jnp.einsum("tc,jc->tj", grad_attn, out_full, preferred_element_type=jnp.float32)),
+        "mp",
+        split_axis=1,
+        concat_axis=0,
+        tiled=True,
+    )
     grad_heads3 = grad_heads.reshape(group_rows, local_heads, HEAD_DIM)
 
     def back_block(carried, inputs):
@@ -258,27 +273,18 @@
     )
     triple_sums = jnp.sum(grad_triples.astype(jnp.float32), axis=0)
     grad_qv_local = jnp.stack([triple_sums[0], triple_sums[2]])
-    piece = grad_triples
     grad_norm1 = lax.psum_scatter(
-        jnp.einsum("tcj,dcj->td", piece, qkv_weight, preferred_element_type=jnp.float32),
+        low(jnp.einsum("tcj,dcj->td", grad_triples, qkv_weight, preferred_element_type=jnp.float32)),
         "mp",
         scatter_dimension=0,
         tiled=True,
-    )
+    ).astype(jnp.float32)
+    qkv_sum = lax.psum(low(grad_qkv_local), "dp").astype(jnp.float32)
     norm1_val, norm1_back = jax.vjp(layer_norm, band_hat, norm1_gain, norm1_bias)
     from_norm1, grad_gain1_local, grad_bias1_local = norm1_back(grad_norm1)
     grad_hat = grad_after + from_norm1
-    summed_weights = lax.psum(
-        (
-            grad_qkv_local,
-            grad_qv_local,
-            grad_out_local,
-            grad_up_local,
-            grad_up_bias_local,
-            grad_down_local,
-        ),
-        "dp",
-    )
+    dec_sum = lax.psum(low(grad_dec_local), ("dp", "mp")).astype(jnp.float32)
+    summed_small = lax.psum((grad_qv_local, grad_up_bias_local), "dp")
     shared = lax.psum(
         (
             jnp.sum(grad_hat, axis=0),
@@ -289,7 +295,6 @@
             grad_bias2_local,
             grad_out_bias_local,
             grad_down_bias_local,
-            grad_dec_local,
             grad_dec_bias_local,
             grad_mask_local,
         ),
@@ -303,19 +308,19 @@
         grad_patches,
         shared[2],
         shared[3],
-        summed_weights[0],
-        summed_weights[1],
-        summed_weights[2],
+        qkv_sum,
+        summed_small[0],
+        out_sum,
         shared[6],
         shared[4],
         shared[5],
-        summed_weights[3],
-        summed_weights[4],
-        summed_weights[5],
+        up_sum,
+        summed_small[1],
+        down_sum,
         shared[7],
+        dec_sum,
         shared[8],
         shared[9],
-        shared[10],
     )
 
 

time: 1000 us -> 743 us (0.74)
  waiting for transfers between devices: 668 us -> 366 us
  blocking collectives: 107 us -> 134 us
  other arithmetic: 42.7 us -> 52.9 us
    reduce_scatter x4 -> x5, waiting for transfers between devices: 238 us -> 89.3 us  [the longest x1 42.5 us: per_device(): lax.psum_scatter(low(jnp.einsum('tf,df->td', grad_pre, up_weight, preferr...]
    all_gather x2, waiting for transfers between devices: 86.2 us -> 13.3 us  [the longest x1 13.3 us: per_device(): proj_grad_all = lax.all_gather(grad_proj_low, 'mp', axis=0, tiled=True)]
    psum x2, waiting for transfers between devices: 266 us -> 194 us  [the longest x1 111 us: per_device(): dec_sum = lax.psum(low(grad_dec_local), ('dp', 'mp')).astype(jnp.float32)]
    all_gather x0 -> x2, blocking collectives: none -> 27.1 us  [the longest x1 17 us: gather_rows(): column = lax.all_gather(mine, 'mp', axis=0)]
    all_gather x1, waiting for transfers between devices: 34.7 us -> 13.1 us  [per_device(): lax.all_gather(normed1, 'mp', axis=0, tiled=True)]
    all_gather x1, waiting for transfers between devices: 24.7 us -> 42.9 us  [per_device(): norm2_all = lax.all_gather(normed2, 'mp', axis=0, tiled=True)]
    unnamed x130 -> x114, local copies, waits for them, and re-layouts: 22.6 us -> 5.4 us
    all_to_all x0 -> x2, waiting for transfers between devices: none -> 13.2 us  [the longest x1 8.1 us: per_device(): lax.all_to_all(heads_out, 'mp', split_axis=0, concat_axis=1, tiled=True)]
  transfers between devices with their start and end apart: 12 -> 15, of which waited for: 12 -> 10; matrix products, arithmetic and copies ran while one was open for 6% -> 19% of each run, Pallas kernels for 0% -> 0%
where the time goes in v1:
time: 743 us; the launch traced here: 734 us
  waiting for transfers between devices  366 us (49%)
  blocking collectives  134 us (18%)
  matrix products  111 us (15%)
  other arithmetic  52.9 us (7%)
  local copies, waits for them, and re-layouts  30.1 us (4%)
  starting transfers between devices  16.5 us (2%)
  between operations  15.1 us (2%)
  loops' own time  8.16 us (1%)
    psum x1, waiting for transfers between devices, per_device(): dec_sum = lax.psum(low(grad_dec_local), ('dp', 'mp')).astype(jnp.float32)  111 us
    psum x1, waiting for transfers between devices, per_device(): qkv_sum = lax.psum(low(grad_qkv_local), 'dp').astype(jnp.float32)  82.7 us
    all_gather x1, waiting for transfers between devices, per_device(): norm2_all = lax.all_gather(normed2, 'mp', axis=0, tiled=True)  42.9 us
    reduce_scatter x1, waiting for transfers between devices, per_device(): lax.psum_scatter(low(jnp.einsum('tf,df->td', grad_pre, up_weight, preferr...  42.5 us
    psum x1, blocking collectives, per_device(): lax.psum((jnp.sum(inputs_f, axis=0), jnp.sum(inputs_f * inputs_f, axis=0)...  42.1 us
    psum x1, blocking collectives, per_device(): lax.psum((jnp.sum(grad_hat, axis=0), jnp.sum(grad_hat * band_hat, axis=0)...  40.7 us
    reduce_scatter x1, waiting for transfers between devices, per_device(): lax.psum_scatter(low(jnp.einsum('tcj,dcj->td', grad_triples, qkv_weight,...  33 us
    all_gather x1, blocking collectives, gather_rows(): column = lax.all_gather(mine, 'mp', axis=0)  17 us
  transfers between devices with their start and end apart: 15, of which 10 were waited for; matrix products, arithmetic and copies ran while one was open for 19% of the time, Pallas kernels for 0%

profile of v1, /device:TPU:0, one launch (start us, length us, event | category | flops | bytes accessed | tf_op | source)
XLA Modules:
  0.0 733.7 jit_solution(15494136100213632518)
XLA Ops:
  8.6 42.1 %all-reduce.1 = (f32[1024]{0:T(1024)S(1)}, f32[1024]{0:T(1024)S(1)}) all-reduce(f32[1024]{0:T(1024)S(1)} %get-tuple-element.181, f32[1024]{0:T(1024)S(1)} %get-tuple-element.180), channel_id=1, replica_groups=mesh['dp'=8,'mp'=4] {'dp','mp'}, use_global_device_ids=true, to_apply=%region_6.7 | all-reduce | flops 2048 | bytes 16384 | tf_op jit(solution)/shard_map/psum | solution.py:74
  55.6 3.0 fusion.56
  58.6 4.1 all-to-all-start.2
  63.7 17.0 %all-gather = bf16[128,1024]{1,0:T(8,128)(2,1)} all-gather(bf16[32,1024]{1,0:T(8,128)(2,1)S(1)} %constant_dynamic-slice_fusion), channel_id=2, replica_groups=mesh['dp'=8,'mp'=4] {'mp'}, dimensions={0}, use_global_device_ids=true | all-gather | bytes 327680 | tf_op jit(solution)/shard_map/all_gather | solution.py:27
  80.8 10.5 %all-gather.3 = s32[4,1,256]{2,1,0:T(1,128)S(1)} all-gather(s32[1,1,256]{2,1,0:T(1,128)S(1)} %bitcast.166), channel_id=1, replica_groups=mesh['dp'=8,'mp'=4] {'mp'}, dimensions={0}, use_global_device_ids=true | all-gather | bytes 5120 | tf_op jit(solution)/shard_map/all_gather | solution.py:84
  92.4 13.1 %all-gather.9.cloned.1.call-done = bf16[1024,1024]{1,0:T(8,128)(2,1)} async-done(((bf16[256,1024]{1,0:T(8,128)(2,1)}), bf16[1024,1024]{1,0:T(8,128)(2,1)}) %all-gather.9.cloned.1.call-update) | async-done | bytes 2097168 | tf_op jit(solution)/shard_map/all_gather | solution.py:83
  105.5 3.9 add_convert_fusion.1
  111.2 22.3 %while.27 = (s32[]{:T(128)}, bf16[2,512,4,64]{1,3,2,0:T(8,128)(2,1)}, f32[2,4,512]{2,1,0:T(4,128)S(1)}, s32[2]{0:T(128)S(1)}, s32[1024]{0:T(1024)S(1)}, /*index=...) while((s32[]{:T(128)}, ...), condition=%wide.region_12.13_spmd, body=%wide.region_9.12_spmd.sunk | while | flops 562690048 | bytes 35203332 | solution.py:116
  118.5 3.0 fusion.170
  129.7 3.0 fusion.170
  136.7 2.9 all_to_all.32
  141.5 4.1 all-to-all-start
  146.2 2.7 fusion.102
  149.0 3.2 copy.77
  152.2 8.1 %all-to-all-done = bf16[4,256,256]{1,2,0:T(8,128)(2,1)} async-done(((bf16[4,256,256]{1,2,0:T(8,128)(2,1)}), bf16[4,256,256]{1,2,0:T(8,128)(2,1)}, u32[]{:S(2)}, u32[]{:S(2)}) %all-to-all-start) | async-done | bytes 524320 | tf_op jit(solution)/shard_map/all_to_all | solution.py:118
  165.1 13.3 %all-gather.13.cloned.1.call-done = bf16[1024,512]{1,0:T(8,128)(2,1)} async-done(((bf16[256,512]{1,0:T(8,128)(2,1)}), bf16[1024,512]{1,0:T(8,128)(2,1)}) %all-gather.13.cloned.1.call-update) | async-done | bytes 1048592 | tf_op jit(solution)/shard_map/all_gather | solution.py:181
  178.3 4.1 convolution_convert_fusion.4
  182.5 42.9 %all-gather.11.cloned.1.call-done = bf16[1024,1024]{1,0:T(8,128)(2,1)} async-done(((bf16[256,1024]{1,0:T(8,128)(2,1)}), bf16[1024,1024]{1,0:T(8,128)(2,1)}) %all-gather.11.cloned.1.call-update) | async-done | bytes 2097168 | tf_op jit(solution)/shard_map/all_gather | solution.py:122
  225.4 4.7 fusion.106
  230.2 13.9 %convert_reduce_fusion = (f32[1024]{0:T(1024)}, bf16[1024,1024]{1,0:T(8,128)(2,1)S(1)}, f32[1024,1024]{1,0:T(8,128)}) fusion(f32[1024,1024]{1,0:T(8,128)S(1)} %fusion.106, f32[1024]{0:T(1024)S(1)} %convert_element_type.184, bf16[1024,1024]{1,0:T(8,128)(2,1)S(1)} %copy-done.61, bf16[1024,1024]{1,0:T(8,128)(2,1)S(1)} %copy-done), kind=kOutput, calls=%fused_computation.48 | convolution fusion | flops 2226125824 | bytes 14688256 | tf_op jit(solution)/shard_map/tc,fc->tf/dot_general | solution.py:193
  245.4 3.7 convolution_convert_fusion.3
  249.2 42.5 %reduce-scatter.8.cloned.1.call-done = bf16[256,1024]{1,0:T(8,128)(2,1)} async-done(((bf16[1024,1024]{1,0:T(8,128)(2,1)}), bf16[256,1024]{1,0:T(8,128)(2,1)}) %reduce-scatter.8.cloned.1.call-update) | async-done | bytes 524304 | tf_op jit(solution)/shard_map/reduce_scatter | solution.py:204
  299.0 3.1 convolution_convert_fusion.2
  302.4 4.6 multiply_convert_fusion.1
  312.9 4.4 fusion.107
  317.4 3.8 convolution_convert_fusion
  322.7 3.5 all-to-all-start.3
  326.3 3.1 add_convert_fusion.2
  329.4 6.1 convolution_convert_fusion.1
  335.5 5.1 all-to-all-done.3
  343.9 30.4 %while.28 = (s32[]{:T(128)}, f32[1024,4,64]{0,2,1:T(8,128)S(1)}, f32[1024,4,64]{0,2,1:T(8,128)}, bf16[2,512,4,64]{1,3,2,0:T(8,128)(2,1)}, s32[2]{0:T(128)S(1)}, ...) while((s32[]{:T(128)}, f32[1024,4,64]{0,2,1:T(8,128)S(1)}, ...), condition=%wide.region_21.22_spmd.clone, body=%wide.region_19.21_spmd.clone.sunk | while | flops 1375729664 | bytes 84740432 | solution.py:260
  351.1 3.3 multiply_reduce_fusion.3
  366.2 3.3 multiply_reduce_fusion.3
  378.7 4.6 fusion.50
  384.0 4.6 bitcast_convert_fusion
  388.7 2.8 convolution_convert_fusion.8
  391.5 3.7 all-to-all-start.1
  396.7 111.1 %all-reduce.7.cloned.1.call-done = bf16[1024,512]{1,0:T(8,128)(2,1)} async-done(((bf16[1024,512]{1,0:T(8,128)(2,1)}), bf16[1024,512]{1,0:T(8,128)(2,1)}) %all-reduce.7.cloned.1.call-update) | async-done | bytes 1048592 | tf_op jit(solution)/shard_map/psum | solution.py:286
  507.8 2.8 convert_element_type.221
  510.7 3.1 add_convert_fusion.3
  514.0 13.4 %all-reduce.2 = (f32[2,256]{1,0:T(2,128)}, f32[1024]{0:T(1024)}) all-reduce(f32[2,256]{1,0:T(2,128)S(1)} %pad_maximum_fusion.2, f32[1024]{0:T(1024)S(1)} %copy-done.49), channel_id=1, replica_groups=mesh['dp'=8,'mp'=4] {'dp'}, use_global_device_ids=true, to_apply=%region_35.36 | all-reduce | flops 1536 | bytes 12288 | tf_op jit(solution)/shard_map/psum | solution.py:287
  527.4 82.7 %all-reduce.9.cloned.1.call-done = (bf16[1024,3,256]{2,0,1:T(8,128)(2,1)}, bf16[1024,1024]{1,0:T(8,128)(2,1)}, bf16[1024,1024]{1,0:T(8,128)(2,1)}) async-done(((bf16[1024,3,256]{2,0,1:T(8,128)(2,1)}, bf16[1024,1024]{1,0:T(8,128)(2,1)}, bf16[1024,1024]{1,0:T(8,128)(2,1)}), (bf16[1024,3,256]{2,0,1:T(8,128)(2,1)}, bf16[1024,1024]{1,0:T(8,128)(2,1)}, bf16[1024,1024]{1,0:T(8,128)(2,1)})) %all-reduce.9.cloned.1.call-update) | async-done | bytes 5767184 | tf_op jit(solution)/shard_map/psum | solution.py:282
  610.2 3.5 convert_element_type.208
  618.7 13.7 %reduce-scatter.14.cloned.1.call-done = bf16[1,32,1024]{2,1,0:T(8,128)(2,1)} async-done(((bf16[4,32,1024]{2,1,0:T(8,128)(2,1)}), bf16[1,32,1024]{2,1,0:T(8,128)(2,1)}) %reduce-scatter.14.cloned.1.call-update) | async-done | bytes 65552 | tf_op jit(solution)/shard_map/reduce_scatter | solution.py:220
  632.4 10.1 %all-gather.2 = bf16[1,256,1024]{2,1,0:T(8,128)(2,1)S(1)} all-gather(bf16[1,32,1024]{2,1,0:T(8,128)(2,1)} %reduce-scatter.14.cloned.1.call-done), channel_id=4, replica_groups=mesh['dp'=8,'mp'=4] {'dp'}, dimensions={1}, use_global_device_ids=true | all-gather | bytes 589824 | tf_op jit(solution)/shard_map/all_gather | solution.py:221
  643.5 33.0 %reduce-scatter.10.cloned.1.call-done = bf16[256,1024]{1,0:T(8,128)(2,1)} async-done(((bf16[1024,1024]{1,0:T(8,128)(2,1)}), bf16[256,1024]{1,0:T(8,128)(2,1)}) %reduce-scatter.10.cloned.1.call-update) | async-done | bytes 524304 | tf_op jit(solution)/shard_map/reduce_scatter | solution.py:276
  680.0 3.6 fusion.97
  683.7 40.7 %all-reduce = (f32[1024]{0:T(1024)S(1)}, f32[1024]{0:T(1024)S(1)}, f32[1024]{0:T(1024)}, f32[1024]{0:T(1024)}, f32[1024]{0:T(1024)}, /*index=5*/f32[1024]{0:T(10...) all-reduce(f32[1024]{0:T(1024)S(1)} %get-tuple-element.176, ...), channel_id=1, replica_groups=mesh['dp'=8,'mp'=4] {'dp','mp'}, use_global_device_ids=true, to_apply=%region_28.29 | all-reduce | flops 9216 | bytes 73728 | tf_op jit(solution)/shard_map/psum | solution.py:288
  (263 shorter events, 90.9 us)
Async XLA Ops:
  7.2 222.9 %copy-start = (bf16[1024,1024]{1,0:T(8,128)(2,1)S(1)}, bf16[1024,1024]{1,0:T(8,128)(2,1)}, u32[]{:S(2)}) copy-start(bf16[1024,1024]{1,0:T(8,128)(2,1)} %param.39) | copy-start | bytes 6291460
  7.2 73.6 %copy-start.52 = (f32[2,256]{1,0:T(2,128)S(1)}, f32[2,256]{1,0:T(2,128)}, u32[]{:S(2)}) copy-start(f32[2,256]{1,0:T(2,128)} %param.32) | copy-start | bytes 6148
  7.2 73.6 %copy-start.53 = (s32[256]{0:T(256)S(1)}, s32[256]{0:T(256)}, u32[]{:S(2)}) copy-start(s32[256]{0:T(256)} %param.26) | copy-start | bytes 3076
  7.2 84.1 %copy-start.43 = (s32[256]{0:T(256)S(1)}, s32[256]{0:T(256)}, u32[]{:S(2)}) copy-start(s32[256]{0:T(256)} %param.27) | copy-start | bytes 3076
  7.2 98.2 %all-gather.9.cloned.1.call-start = ((), (), s32[]{:S(2)}) async-start(), calls=%async_computation.9 | async-start | bytes 2621440 | tf_op jit(solution)/shard_map/all_gather | solution.py:83
  50.7 109.6 %copy-start.27 = (f32[1024]{0:T(1024)}, f32[1024]{0:T(1024)S(1)}, u32[]{:S(2)}) copy-start(f32[1024]{0:T(1024)S(1)} %get-tuple-element.257) | copy-start | bytes 12292
  50.7 109.6 %copy-start.29 = (f32[1024]{0:T(1024)}, f32[1024]{0:T(1024)S(1)}, u32[]{:S(2)}) copy-start(f32[1024]{0:T(1024)S(1)} %get-tuple-element.258) | copy-start | bytes 12292
  52.0 10.8 %copy-start.33 = (f32[256]{0:T(256)}, f32[256]{0:T(256)S(1)}, u32[]{:S(2)}) copy-start(f32[256]{0:T(256)S(1)} %broadcast_multiply_fusion.4) | copy-start | bytes 3076
  53.4 9.4 %copy-start.41 = (f32[256]{0:T(256)}, f32[256]{0:T(256)S(1)}, u32[]{:S(2)}) copy-start(f32[256]{0:T(256)S(1)} %fusion.76) | copy-start | bytes 3076
  58.6 82.9 %all-to-all-start.2 = ((bf16[8,64,512]{2,1,0:T(8,128)(2,1)}), bf16[8,64,512]{2,1,0:T(8,128)(2,1)}, u32[]{:S(2)}, u32[]{:S(2)}) async-start(bf16[8,64,512]{2,1,0:T(8,128)(2,1)} %bitcast.21), calls=%async_computation.3 | async-start | bytes 1048576 | tf_op jit(solution)/shard_map/all_to_all | solution.py:158
  62.8 86.2 %all-gather.15.cloned.1.call-start = ((), (), s32[]{:S(2)}) async-start(), calls=%async_computation.18 | async-start | bytes 2359296 | tf_op jit(solution)/shard_map/all_gather | solution.py:28
  136.7 23.6 %copy-start.2 = (bf16[256,1024]{1,0:T(8,128)(2,1)S(1)}, bf16[256,1024]{1,0:T(8,128)(2,1)}, u32[]{:S(2)}) copy-start(bf16[256,1024]{1,0:T(8,128)(2,1)} %param.25) | copy-start | bytes 1572868
  136.7 23.6 %copy-start.35 = (f32[1024]{0:T(1024)S(1)}, f32[1024]{0:T(1024)}, u32[]{:S(2)}) copy-start(f32[1024]{0:T(1024)} %param.34) | copy-start | bytes 12292
  141.5 18.8 %all-to-all-start = ((bf16[4,256,256]{1,2,0:T(8,128)(2,1)}), bf16[4,256,256]{1,2,0:T(8,128)(2,1)}, u32[]{:S(2)}, u32[]{:S(2)}) async-start(bf16[4,256,256]{1,2,0:T(8,128)(2,1)} %copy.76), calls=%async_computation | async-start | bytes 1048576 | tf_op jit(solution)/shard_map/all_to_all | solution.py:118
  145.7 32.7 %all-gather.13.cloned.1.call-start = ((), (), s32[]{:S(2)}) async-start(), calls=%async_computation.12 | async-start | bytes 1310720 | tf_op jit(solution)/shard_map/all_gather | solution.py:181
  148.9 76.5 %all-gather.11.cloned.1.call-start = ((), (), s32[]{:S(2)}) async-start(), calls=%async_computation.10 | async-start | bytes 2621440 | tf_op jit(solution)/shard_map/all_gather | solution.py:122
  149.0 14.9 %copy-start.32 = (f32[1024]{0:T(1024)S(1)}, f32[1024]{0:T(1024)}, u32[]{:S(2)}) copy-start(f32[1024]{0:T(1024)} %param.35) | copy-start | bytes 12292
  149.0 14.9 %copy-start.46 = (f32[1024]{0:T(1024)S(1)}, f32[1024]{0:T(1024)}, u32[]{:S(2)}) copy-start(f32[1024]{0:T(1024)} %param.36) | copy-start | bytes 12292
  152.2 12.8 %copy-start.50 = (bf16[1024]{0:T(1024)(128)(2,1)S(1)}, bf16[1024]{0:T(1024)(128)(2,1)}, u32[]{:S(2)}) copy-start(bf16[1024]{0:T(1024)(128)(2,1)} %param.38) | copy-start | bytes 6148
  165.0 126.7 %reduce-scatter.8.cloned.1.call-start = ((), (), s32[]{:S(2)}) async-start(), calls=%async_computation.13 | async-start | bytes 2621440 | tf_op jit(solution)/shard_map/reduce_scatter | solution.py:204
  230.1 14.0 %copy-start.13 = (f32[1024,1024]{1,0:T(8,128)}, f32[1024,1024]{1,0:T(8,128)S(1)}, u32[]{:S(2)}) copy-start(f32[1024,1024]{1,0:T(8,128)S(1)} %fusion.106) | copy-start | bytes 12582916
  230.1 15.3 %copy-start.56 = (bf16[1024,1024]{1,0:T(8,128)(2,1)S(1)}, bf16[1024,1024]{1,0:T(8,128)(2,1)}, u32[]{:S(2)}) copy-start(bf16[1024,1024]{1,0:T(8,128)(2,1)} %param.37) | copy-start | bytes 6291460
  249.1 47.8 %copy-start.14 = (bf16[256,512]{1,0:T(8,128)(2,1)S(1)}, bf16[256,512]{1,0:T(8,128)(2,1)}, u32[]{:S(2)}) copy-start(bf16[256,512]{1,0:T(8,128)(2,1)} %get-tuple-element.254) | copy-start | bytes 786436
  249.2 134.2 %reduce-scatter.12.cloned.1.call-start = ((), (), s32[]{:S(2)}) async-start(), calls=%async_computation.15 | async-start | bytes 2359296 | tf_op jit(solution)/shard_map/reduce_scatter | solution.py:219
  302.1 86.6 %reduce-scatter.6.cloned.1.call-start = ((), (), s32[]{:S(2)}) async-start(), calls=%async_computation.11 | async-start | bytes 1310720 | tf_op jit(solution)/shard_map/reduce_scatter | solution.py:129
  322.7 17.9 %all-to-all-start.3 = ((bf16[256,4,256]{2,0,1:T(8,128)(2,1)}), bf16[256,4,256]{2,0,1:T(8,128)(2,1)S(1)}, u32[]{:S(2)}, u32[]{:S(2)}) async-start(bf16[256,4,256]{2,0,1:T(8,128)(2,1)} %bitcast.160), calls=%async_computation.5 | async-start | bytes 1048576 | tf_op jit(solution)/shard_map/all_to_all | solution.py:222
  326.2 181.6 %all-reduce.7.cloned.1.call-start = ((), (), s32[]{:S(2)}) async-start(), calls=%async_computation.17 | async-start | bytes 2097152 | tf_op jit(solution)/shard_map/psum | solution.py:286
  329.4 14.6 %copy-start.5 = (bf16[1024,4,64]{0,2,1:T(8,128)(2,1)S(1)}, bf16[1024,4,64]{0,2,1:T(8,128)(2,1)}, u32[]{:S(2)}) copy-start(bf16[1024,4,64]{0,2,1:T(8,128)(2,1)} %copy-done.4) | copy-start | bytes 1572868
  329.4 14.5 %copy-start.10 = (bf16[1024,4,64]{0,2,1:T(8,128)(2,1)S(1)}, bf16[1024,4,64]{0,2,1:T(8,128)(2,1)}, u32[]{:S(2)}) copy-start(bf16[1024,4,64]{0,2,1:T(8,128)(2,1)} %get-tuple-element.484) | copy-start | bytes 1572868
  329.4 280.8 %all-reduce.9.cloned.1.call-start = ((), (), s32[]{:S(2)}) async-start(), calls=%async_computation.19 | async-start | bytes 11534336 | tf_op jit(solution)/shard_map/psum | solution.py:282
  383.3 249.0 %reduce-scatter.14.cloned.1.call-start = ((), (), s32[]{:S(2)}) async-start(), calls=%async_computation.16 | async-start | bytes 327680 | tf_op jit(solution)/shard_map/reduce_scatter | solution.py:220
  384.0 292.6 %reduce-scatter.10.cloned.1.call-start = ((), (), s32[]{:S(2)}) async-start(), calls=%async_computation.14 | async-start | bytes 2621440 | tf_op jit(solution)/shard_map/reduce_scatter | solution.py:276
  388.7 122.0 %copy-start.59 = (f32[512]{0:T(512)S(1)}, f32[512]{0:T(512)}, u32[]{:S(2)}) copy-start(f32[512]{0:T(512)} %param.43) | copy-start | bytes 6148
  391.5 119.2 %all-to-all-start.1 = ((bf16[8,64,512]{2,1,0:T(8,128)(2,1)}), bf16[8,64,512]{2,1,0:T(8,128)(2,1)S(1)}, u32[]{:S(2)}, u32[]{:S(2)}) async-start(bf16[8,64,512]{2,1,0:T(8,128)(2,1)} %bitcast.19), calls=%async_computation.2 | async-start | bytes 1048576 | tf_op jit(solution)/shard_map/all_to_all | solution.py:151
  396.7 117.3 %copy-start.49 = (f32[1024]{0:T(1024)S(1)}, f32[1024]{0:T(1024)}, u32[]{:S(2)}) copy-start(f32[1024]{0:T(1024)} %get-tuple-element.237) | copy-start | bytes 12292
  616.1 60.4 %copy-start.3 = (bf16[256,1024]{1,0:T(8,128)(2,1)S(1)}, bf16[256,1024]{1,0:T(8,128)(2,1)}, u32[]{:S(2)}) copy-start(bf16[256,1024]{1,0:T(8,128)(2,1)} %param.25) | copy-start | bytes 1572868
  616.1 60.4 %copy-start.28 = (f32[1024]{0:T(1024)S(1)}, f32[1024]{0:T(1024)}, u32[]{:S(2)}) copy-start(f32[1024]{0:T(1024)} %copy-done.27) | copy-start | bytes 12292
  616.1 60.4 %copy-start.30 = (f32[1024]{0:T(1024)S(1)}, f32[1024]{0:T(1024)}, u32[]{:S(2)}) copy-start(f32[1024]{0:T(1024)} %copy-done.29) | copy-start | bytes 12292
  616.1 60.4 %copy-start.31 = (f32[1024]{0:T(1024)S(1)}, f32[1024]{0:T(1024)}, u32[]{:S(2)}) copy-start(f32[1024]{0:T(1024)} %param.29) | copy-start | bytes 12292
  616.2 60.4 %copy-start.34 = (f32[256]{0:T(256)S(1)}, f32[256]{0:T(256)}, u32[]{:S(2)}) copy-start(f32[256]{0:T(256)} %copy-done.33) | copy-start | bytes 3076
  616.2 62.1 %copy-start.42 = (f32[256]{0:T(256)S(1)}, f32[256]{0:T(256)}, u32[]{:S(2)}) copy-start(f32[256]{0:T(256)} %copy-done.41) | copy-start | bytes 3076
  616.2 62.1 %copy-start.40 = (f32[256]{0:T(256)S(1)}, f32[256]{0:T(256)}, u32[]{:S(2)}) copy-start(f32[256]{0:T(256)} %copy-done.39) | copy-start | bytes 3076
  616.2 63.8 %copy-start.45 = (f32[256]{0:T(256)S(1)}, f32[256]{0:T(256)}, u32[]{:S(2)}) copy-start(f32[256]{0:T(256)} %copy-done.44) | copy-start | bytes 3076
  618.7 65.0 %copy-start.36 = (f32[1024]{0:T(1024)S(1)}, f32[1024]{0:T(1024)}, u32[]{:S(2)}) copy-start(f32[1024]{0:T(1024)} %get-tuple-element.171) | copy-start | bytes 12292
  618.7 65.0 %copy-start.37 = (f32[1024]{0:T(1024)S(1)}, f32[1024]{0:T(1024)}, u32[]{:S(2)}) copy-start(f32[1024]{0:T(1024)} %get-tuple-element.177) | copy-start | bytes 12292
  618.7 65.0 %copy-start.38 = (f32[1024]{0:T(1024)S(1)}, f32[1024]{0:T(1024)}, u32[]{:S(2)}) copy-start(f32[1024]{0:T(1024)} %get-tuple-element.240) | copy-start | bytes 12292
  618.7 65.0 %copy-start.51 = (f32[512]{0:T(512)S(1)}, f32[512]{0:T(512)}, u32[]{:S(2)}) copy-start(f32[512]{0:T(512)} %get-tuple-element.253) | copy-start | bytes 6148
  676.6 50.2 %copy-start.1 = (bf16[1024,1024]{1,0:T(8,128)(2,1)S(1)}, bf16[1024,1024]{1,0:T(8,128)(2,1)}, u32[]{:S(2)}) copy-start(bf16[1024,1024]{1,0:T(8,128)(2,1)} %param.39) | copy-start | bytes 6291460
  (38 other events, 116.2 us)
Sparse Core Ops, SparseCore 0:
  55.7 49.7 all-gather.8
  107.4 26.6 all-gather.14
  149.0 29.2 all-gather.12
  180.3 45.0 all-gather.10
  249.3 42.4 reduce-scatter.7
  302.3 40.3 reduce-scatter.11
  345.5 27.2 reduce-scatter.5
  378.6 129.2 all-reduce.6
  512.6 97.5 all-reduce.8
  612.3 20.0 reduce-scatter.13
  634.7 41.8 reduce-scatter.9
